TPU v7x, 32 devices: a whole 2x2x4 slice. The times are simulated.
32 devices in a mesh: dp: 8 (over y, x, core), tensor: 4 (over z).
Axes of the slice: x: 2, y: 2, z: 4, core: 2. Of those that a mesh axis runs over, the one named last changes fastest.
Arguments:
- inputs: bfloat16 [16, 1024, 1024], P('dp', 'tensor'), may hold values from -6 to 6
- cotangent: bfloat16 [16, 1024, 1024], P('dp', 'tensor'), may hold values from -6 to 6
- lengths: int32 [16], P('dp'), may hold values from 1 to 1024, as said below
- block_ids: int32 [16, 1024], P('dp'), may hold values from 0 to 7, never falling along the last dimension, each value on 1 to 256 neighbouring positions
- ln1_gain: float32 [1024], replicated, may hold values from 0.5 to 1.5
- ln1_bias: float32 [1024], replicated, may hold values from -1 to 1
- ln2_gain: float32 [1024], replicated, may hold values from 0.5 to 1.5
- ln2_bias: float32 [1024], replicated, may hold values from -1 to 1
- w_qkv: bfloat16 [1024, 3072], P('dp', 'tensor'), may hold values from -0.1875 to 0.1875
- b_qkv: float32 [3072], P('tensor'), may hold values from -1 to 1
- w_out: bfloat16 [1024, 1024], P('dp', 'tensor'), may hold values from -1 to 1
- b_out: float32 [1024], replicated, may hold values from -1 to 1
- w_up: bfloat16 [1024, 4096], P('dp', 'tensor'), may hold values from -0.1875 to 0.1875
- b_up: float32 [4096], P('tensor'), may hold values from -1 to 1
- w_down: bfloat16 [1024, 4096], P('dp', 'tensor'), may hold values from -0.09375 to 0.09375
- b_down: float32 [1024], replicated, may hold values from -1 to 1
Outputs:
- layer_out: bfloat16 [16, 1024, 1024], P('dp', 'tensor')
- grad_inputs: float32 [16, 1024, 1024], P('dp', 'tensor')
- grad_w_qkv: float32 [1024, 3072], P('dp', 'tensor')
- grad_w_out: float32 [1024, 1024], P('dp', 'tensor')
- grad_w_up: float32 [1024, 4096], P('dp', 'tensor')
- grad_w_down: float32 [1024, 4096], P('dp', 'tensor')
- grad_b_qkv: float32 [3072], P('tensor')
- grad_b_up: float32 [4096], P('tensor')
- grad_ln1_gain: float32 [1024], replicated
- grad_ln1_bias: float32 [1024], replicated
- grad_ln2_gain: float32 [1024], replicated
- grad_ln2_bias: float32 [1024], replicated
- grad_b_out: float32 [1024], replicated
- grad_b_down: float32 [1024], replicated
Inputs may be any that keep to these rules, and one draw needn't show every extreme that they name: `lengths`: live tokens of each sequence, at its start; keys from the length on are padding; some sequence has all 1024 live. `block_ids`: along each sequence the block number starts at 0 and never falls; each block spans 1 to 256 consecutive positions and some block spans exactly 256.
All inputs are finite; a program needn't handle non-finite values.
Results may differ from a plain program's by a relative error of at most 0.0098.
Values may be sent and summed in bfloat16 or wider, within the bound.
A program may use at most 256 MiB of HBM per device.

v0:
```python
import jax
import jax.numpy as jnp
from jax import lax
from jax.sharding import PartitionSpec as P

HEAD = 64
ROT = 16
BLOCK = 256
MICRO = 2


def layer_norm(values, ln_gain, ln_bias):
    centre = jnp.mean(values, axis=-1, keepdims=True)
    shifted = values - centre
    spread = jnp.mean(shifted * shifted, axis=-1, keepdims=True)
    return shifted * lax.rsqrt(spread + 1e-05) * ln_gain + ln_bias


def rope_tables(length, rotary):
    halved = rotary // 2
    frequency = 1.0 / 10000.0 ** (jnp.arange(halved, dtype=jnp.float32) * (2.0 / rotary))
    angles = jnp.arange(length, dtype=jnp.float32)[:, None] * frequency[None, :]
    angles = jnp.concatenate([angles, angles], axis=1)[:, None, :]
    return (jnp.cos(angles), jnp.sin(angles))


def rotate(head_rows, cos_table, sin_table, rotary):
    halved = rotary // 2
    moving = head_rows[..., :rotary]
    turned = jnp.concatenate([-moving[..., halved:], moving[..., :halved]], axis=-1)
    moving = moving * cos_table + turned * sin_table
    return jnp.concatenate([moving, head_rows[..., rotary:]], axis=-1)


def visible(block_rows, limits, first_row, tile_rows, key_end):
    own_ids = block_rows[:, first_row : first_row + tile_rows]
    key_pos = jnp.arange(key_end, dtype=jnp.int32)
    allowed = (block_rows[:, None, :key_end] <= own_ids[:, :, None]) & (
        key_pos[None, None, :] < limits[:, None, None]
    )
    return allowed[:, None]


def gelu_exact(argument):
    return jax.nn.gelu(argument, approximate=False)


def on_device(
    inputs,
    cotangent,
    lengths,
    block_ids,
    ln1_gain,
    ln1_bias,
    ln2_gain,
    ln2_bias,
    w_qkv,
    b_qkv,
    w_out,
    b_out,
    w_up,
    b_up,
    w_down,
    b_down,
):
    model_width = inputs.shape[2]
    per_micro = inputs.shape[0] // MICRO
    length = block_ids.shape[1]
    tile_rows = min(512, length)
    heads_here = w_qkv.shape[1] // (3 * HEAD)
    scaling = HEAD ** (-0.5)
    cos_table, sin_table = rope_tables(length, ROT)
    grad_qkv = jnp.zeros((model_width, w_qkv.shape[1]), jnp.float32)
    grad_outw = jnp.zeros((model_width, w_out.shape[1]), jnp.float32)
    grad_upw = jnp.zeros((model_width, w_up.shape[1]), jnp.float32)
    grad_downw = jnp.zeros((model_width, w_down.shape[1]), jnp.float32)
    sum_bias_qkv = jnp.zeros((w_qkv.shape[1],), jnp.float32)
    sum_bias_up = jnp.zeros((w_up.shape[1],), jnp.float32)
    sum_gain_one = jnp.zeros((model_width,), jnp.float32)
    sum_bias_one = jnp.zeros((model_width,), jnp.float32)
    sum_gain_two = jnp.zeros((model_width,), jnp.float32)
    sum_bias_two = jnp.zeros((model_width,), jnp.float32)
    sum_slope = jnp.zeros((model_width,), jnp.float32)
    out_rows = []
    grad_rows = []
    tile_starts = list(range(0, length, tile_rows))
    key_ends = [min(length, first_row + tile_rows + BLOCK) for first_row in tile_starts]
    for micro_idx in range(MICRO):
        first_seq = micro_idx * per_micro
        last_seq = first_seq + per_micro
        residual = inputs[first_seq:last_seq].astype(jnp.float32)
        limits = lengths[first_seq:last_seq]
        block_rows = block_ids[first_seq:last_seq]
        value_one, norm_one_back = jax.vjp(layer_norm, residual, ln1_gain, ln1_bias)
        value_two, norm_two_back = jax.vjp(layer_norm, residual, ln2_gain, ln2_bias)
        whole_one, whole_two = (
            lax.all_gather(value_one.astype(jnp.bfloat16), "tensor", axis=1, tiled=True),
            lax.all_gather(value_two.astype(jnp.bfloat16), "tensor", axis=1, tiled=True),
        )
        qkv_full, out_full, up_full, down_full = (
            lax.all_gather(w_qkv, "dp", axis=0, tiled=True),
            lax.all_gather(w_out, "dp", axis=0, tiled=True),
            lax.all_gather(w_up, "dp", axis=0, tiled=True),
            lax.all_gather(w_down, "dp", axis=0, tiled=True),
        )
        projected = (
            jnp.einsum("bsd,dc->bsc", whole_one, qkv_full, preferred_element_type=jnp.float32)
            + b_qkv
        )
        projected = projected.reshape(per_micro, length, heads_here, 3, HEAD)
        queries = rotate(projected[:, :, :, 0], cos_table, sin_table, ROT).astype(jnp.bfloat16)
        key_rows = rotate(projected[:, :, :, 1], cos_table, sin_table, ROT).astype(jnp.bfloat16)
        values = projected[:, :, :, 2].astype(jnp.bfloat16)
        scaled_q = (queries * jnp.bfloat16(scaling)).transpose(0, 2, 1, 3)
        keys_hd = key_rows.transpose(0, 2, 1, 3)
        values_hd = values.transpose(0, 2, 1, 3)
        log_sums = []
        mixed_parts = []
        for first_row, key_end in zip(tile_starts, key_ends):
            q_block = scaled_q[:, :, first_row : first_row + tile_rows]
            allowed = visible(block_rows, limits, first_row, tile_rows, key_end)
            scores = jnp.einsum(
                "bhqe,bhke->bhqk",
                q_block,
                keys_hd[:, :, :key_end],
                preferred_element_type=jnp.float32,
            )
            scores = jnp.where(allowed, scores, -1e30)
            row_peak = jnp.max(scores, axis=-1)
            powered = jnp.exp(scores - row_peak[..., None])
            totals = jnp.sum(powered, axis=-1)
            soft_low = (powered / totals[..., None]).astype(jnp.bfloat16)
            log_sums.append(row_peak + jnp.log(totals))
            mixed_parts.append(
                jnp.einsum(
                    "bhqk,bhke->bhqe",
                    soft_low,
                    values_hd[:, :, :key_end],
                    preferred_element_type=jnp.float32,
                )
            )
        attended = (
            jnp.concatenate(mixed_parts, axis=2)
            .transpose(0, 2, 1, 3)
            .reshape(per_micro, length, heads_here * HEAD)
            .astype(jnp.bfloat16)
        )
        partial_sum = jnp.einsum(
            "bsf,df->bsd", attended, out_full, preferred_element_type=jnp.float32
        )
        hidden_pre = (
            jnp.einsum("bsd,df->bsf", whole_two, up_full, preferred_element_type=jnp.float32) + b_up
        )
        gelu_value, gelu_back = jax.vjp(gelu_exact, hidden_pre)
        activated = gelu_value.astype(jnp.bfloat16)
        partial_sum = partial_sum + jnp.einsum(
            "bsf,df->bsd", activated, down_full, preferred_element_type=jnp.float32
        )
        reduced = lax.psum_scatter(partial_sum, "tensor", scatter_dimension=1, tiled=True)
        out_rows.append((residual + reduced + b_out + b_down).astype(jnp.bfloat16))
        slope_local = cotangent[first_seq:last_seq]
        slope = lax.all_gather(slope_local, "tensor", axis=1, tiled=True)
        qkv_full, out_full, up_full, down_full = (
            lax.all_gather(w_qkv, "dp", axis=0, tiled=True),
            lax.all_gather(w_out, "dp", axis=0, tiled=True),
            lax.all_gather(w_up, "dp", axis=0, tiled=True),
            lax.all_gather(w_down, "dp", axis=0, tiled=True),
        )
        grad_outw = grad_outw + jnp.einsum(
            "bsd,bsf->df", slope, attended, preferred_element_type=jnp.float32
        )
        grad_downw = grad_downw + jnp.einsum(
            "bsd,bsf->df", slope, activated, preferred_element_type=jnp.float32
        )
        grad_att = jnp.einsum(
            "bsd,df->bsf", slope, out_full, preferred_element_type=jnp.float32
        ).astype(jnp.bfloat16)
        grad_att = grad_att.reshape(per_micro, length, heads_here, HEAD).transpose(0, 2, 1, 3)
        grad_act = jnp.einsum("bsd,df->bsf", slope, down_full, preferred_element_type=jnp.float32)
        grad_hidden = gelu_back(grad_act)[0].astype(jnp.bfloat16)
        grad_upw = grad_upw + jnp.einsum(
            "bsd,bsf->df", whole_two, grad_hidden, preferred_element_type=jnp.float32
        )
        sum_bias_up = sum_bias_up + jnp.sum(grad_hidden.astype(jnp.float32), axis=(0, 1))
        grad_two = jnp.einsum(
            "bsf,df->bsd", grad_hidden, up_full, preferred_element_type=jnp.float32
        )
        grad_keys = jnp.zeros((per_micro, heads_here, length, HEAD), jnp.float32)
        grad_values = jnp.zeros((per_micro, heads_here, length, HEAD), jnp.float32)
        query_parts = []
        for index_tile, first_row in enumerate(tile_starts):
            key_end = key_ends[index_tile]
            q_block = scaled_q[:, :, first_row : first_row + tile_rows]
            g_block = grad_att[:, :, first_row : first_row + tile_rows]
            k_block = keys_hd[:, :, :key_end]
            allowed = visible(block_rows, limits, first_row, tile_rows, key_end)
            scores = jnp.einsum(
                "bhqe,bhke->bhqk", q_block, k_block, preferred_element_type=jnp.float32
            )
            scores = jnp.where(allowed, scores, -1e30)
            soft_full = jnp.exp(scores - log_sums[index_tile][..., None])
            soft_low = soft_full.astype(jnp.bfloat16)
            value_part = jnp.einsum(
                "bhqk,bhqe->bhke", soft_low, g_block, preferred_element_type=jnp.float32
            )
            grad_values = grad_values.at[:, :, :key_end].add(value_part)
            grad_soft = jnp.einsum(
                "bhqe,bhke->bhqk",
                g_block,
                values_hd[:, :, :key_end],
                preferred_element_type=jnp.float32,
            )
            centred = jnp.sum(soft_full * grad_soft, axis=-1)
            grad_scores = (soft_full * (grad_soft - centred[..., None])).astype(jnp.bfloat16)
            query_parts.append(
                jnp.einsum(
                    "bhqk,bhke->bhqe", grad_scores, k_block, preferred_element_type=jnp.float32
                )
                * scaling
            )
            key_part = jnp.einsum(
                "bhqk,bhqe->bhke", grad_scores, q_block, preferred_element_type=jnp.float32
            )
            grad_keys = grad_keys.at[:, :, :key_end].add(key_part)
        grad_queries = jnp.concatenate(query_parts, axis=2).transpose(0, 2, 1, 3)
        grad_keys = grad_keys.transpose(0, 2, 1, 3)
        grad_values = grad_values.transpose(0, 2, 1, 3)
        grad_projected = jnp.stack(
            [
                rotate(grad_queries, cos_table, -sin_table, ROT),
                rotate(grad_keys, cos_table, -sin_table, ROT),
                grad_values,
            ],
            axis=3,
        )
        grad_projected = grad_projected.reshape(per_micro, length, 3 * heads_here * HEAD).astype(
            jnp.bfloat16
        )
        grad_qkv = grad_qkv + jnp.einsum(
            "bsd,bsc->dc", whole_one, grad_projected, preferred_element_type=jnp.float32
        )
        sum_bias_qkv = sum_bias_qkv + jnp.sum(grad_projected.astype(jnp.float32), axis=(0, 1))
        grad_one = jnp.einsum(
            "bsc,dc->bsd", grad_projected, qkv_full, preferred_element_type=jnp.float32
        )
        slope_rows = slope_local.astype(jnp.float32)
        back_one, back_two = (
            lax.psum_scatter(grad_one, "tensor", scatter_dimension=1, tiled=True),
            lax.psum_scatter(grad_two, "tensor", scatter_dimension=1, tiled=True),
        )
        input_one, gain_one, bias_one = norm_one_back(back_one)
        input_two, gain_two, bias_two = norm_two_back(back_two)
        grad_rows.append(slope_rows + input_one + input_two)
        sum_gain_one = sum_gain_one + gain_one
        sum_bias_one = sum_bias_one + bias_one
        sum_gain_two = sum_gain_two + gain_two
        sum_bias_two = sum_bias_two + bias_two
        sum_slope = sum_slope + jnp.sum(slope_rows, axis=(0, 1))
    reduced_grads = (
        lax.psum_scatter(grad_qkv, "dp", scatter_dimension=0, tiled=True),
        lax.psum_scatter(grad_outw, "dp", scatter_dimension=0, tiled=True),
        lax.psum_scatter(grad_upw, "dp", scatter_dimension=0, tiled=True),
        lax.psum_scatter(grad_downw, "dp", scatter_dimension=0, tiled=True),
    )
    bias_qkv_total, bias_up_total = lax.psum((sum_bias_qkv, sum_bias_up), "dp")
    shared = lax.psum(
        (sum_gain_one, sum_bias_one, sum_gain_two, sum_bias_two, sum_slope), ("dp", "tensor")
    )
    return (
        jnp.concatenate(out_rows, axis=0),
        jnp.concatenate(grad_rows, axis=0),
        reduced_grads[0],
        reduced_grads[1],
        reduced_grads[2],
        reduced_grads[3],
        bias_qkv_total,
        bias_up_total,
        shared[0],
        shared[1],
        shared[2],
        shared[3],
        shared[4],
        shared[4],
    )


def solution(mesh):
    in_specs = (
        P("dp", "tensor", None),
        P("dp", "tensor", None),
        P("dp"),
        P("dp", None),
        P(),
        P(),
        P(),
        P(),
        P("dp", "tensor"),
        P("tensor"),
        P("dp", "tensor"),
        P(),
        P("dp", "tensor"),
        P("tensor"),
        P("dp", "tensor"),
        P(),
    )
    out_specs = (
        P("dp", "tensor", None),
        P("dp", "tensor", None),
        P("dp", "tensor"),
        P("dp", "tensor"),
        P("dp", "tensor"),
        P("dp", "tensor"),
        P("tensor"),
        P("tensor"),
        P(),
        P(),
        P(),
        P(),
        P(),
        P(),
    )
    return jax.shard_map(
        on_device, mesh=mesh, in_specs=in_specs, out_specs=out_specs, check_vma=False
    )
```

profile of v0, /device:TPU:0, one launch (start us, length us, event | category | flops | bytes accessed | tf_op | source)
XLA Modules:
  0.0 1063.5 jit_solution(9621609152329100266)
XLA Ops:
  11.7 3.2 fusion.173
  24.5 12.7 %all_gather.44 = bf16[1024,256]{1,0:T(8,128)(2,1)S(1)} all-gather(bf16[128,256]{1,0:T(8,128)(2,1)S(1)} %copy-done.88), channel_id=1, replica_groups=mesh['dp'=8,'tensor'=4] {'dp'}, dimensions={0}, use_global_device_ids=true | all-gather | bytes 589824 | tf_op jit(solution)/shard_map/all_gather | solution.py:102
  39.7 48.1 %all-gather.10.cloned.1.call-done = bf16[1,1024,1024]{2,1,0:T(8,128)(2,1)} async-done(((bf16[1,256,1024]{2,1,0:T(8,128)(2,1)}), bf16[1,1024,1024]{2,1,0:T(8,128)(2,1)}) %all-gather.10.cloned.1.call-update) | async-done | bytes 2097168 | tf_op jit(solution)/shard_map/all_gather | solution.py:97
  87.8 3.9 fusion.85
  96.9 37.2 %all-gather.20.cloned.1.call-done = bf16[1,1024,1024]{2,1,0:T(8,128)(2,1)} async-done(((bf16[1,256,1024]{2,1,0:T(8,128)(2,1)}), bf16[1,1024,1024]{2,1,0:T(8,128)(2,1)}) %all-gather.20.cloned.1.call-update) | async-done | bytes 2097168 | tf_op jit(solution)/shard_map/all_gather | solution.py:97
  134.1 3.9 fusion.91
  147.8 2.8 fusion.161
  150.5 29.7 %all-gather.24.cloned.1.call-done = bf16[1,1024,1024]{2,1,0:T(8,128)(2,1)} async-done(((bf16[1,256,1024]{2,1,0:T(8,128)(2,1)}), bf16[1,1024,1024]{2,1,0:T(8,128)(2,1)}) %all-gather.24.cloned.1.call-update) | async-done | bytes 2097168 | tf_op jit(solution)/shard_map/all_gather | solution.py:162
  180.2 2.3 fusion.142
  182.6 4.8 multiply_reduce_fusion.3
  194.4 2.2 fusion
  197.7 3.6 fusion.155
  202.8 2.1 fusion.3
  205.0 2.0 fusion.160
  208.6 2.3 fusion.1
  212.0 3.8 fusion.154
  215.9 10.4 all-gather.26.cloned.1.call-done
  226.3 3.3 fusion.145
  229.6 2.4 fusion.46
  234.4 6.3 multiply_reduce_fusion.1
  240.8 2.3 multiply_convert_fusion.1
  243.2 2.2 fusion.158
  247.4 2.6 multiply_reduce_fusion.2
  251.7 21.3 %all-gather.22.cloned.1.call-done = bf16[1,1024,1024]{2,1,0:T(8,128)(2,1)} async-done(((bf16[1,256,1024]{2,1,0:T(8,128)(2,1)}), bf16[1,1024,1024]{2,1,0:T(8,128)(2,1)}) %all-gather.22.cloned.1.call-update) | async-done | bytes 2097168 | tf_op jit(solution)/shard_map/all_gather | solution.py:98
  273.0 28.5 %all-gather.16.cloned.1.call-done = bf16[1024,1024]{1,0:T(8,128)(2,1)} async-done(((bf16[128,1024]{1,0:T(8,128)(2,1)}), bf16[1024,1024]{1,0:T(8,128)(2,1)}) %all-gather.16.cloned.1.call-update) | async-done | bytes 2097168 | tf_op jit(solution)/shard_map/all_gather | solution.py:103
  301.5 6.6 fusion.66
  308.2 41.5 %all-gather.14.cloned.1.call-done = bf16[1,1024,1024]{2,1,0:T(8,128)(2,1)} async-done(((bf16[1,256,1024]{2,1,0:T(8,128)(2,1)}), bf16[1,1024,1024]{2,1,0:T(8,128)(2,1)}) %all-gather.14.cloned.1.call-update) | async-done | bytes 2097168 | tf_op jit(solution)/shard_map/all_gather | solution.py:98
  349.6 23.9 %multiply_convert_fusion.5 = (bf16[1024,1024]{1,0:T(8,128)(2,1)S(1)}, f32[1024,1024]{1,0:T(8,128)}, bf16[1024,1024]{1,0:T(8,128)(2,1)S(1)}, f32[1024,1024]{1,0:T(8,128)}, f32[1024,1024]{1,0:T(8,128)}) fusion(f32[1024]{0:T(1024)} %param.53, f32[1024,1024]{1,0:T(8,128)} %fusion.66, bf16[1024,1024]{1,0:T(8,128)(2,1)} %all-gather.16.cloned.1.call-done, ...), kind=kOutput, calls=%fused_computation.58 | convolution fusion | flops 2285895680 | bytes 25169920 | tf_op jit(solution)/shard_map/bsd,df->bsf/dot_general | solution.py:152
  373.6 2.4 fusion.44
  376.7 4.5 add_bitcast_fusion
  385.4 3.0 fusion.156
  388.4 6.6 multiply_reduce_fusion
  395.1 2.1 multiply_convert_fusion
  405.4 2.2 fusion.139
  409.1 3.9 convolution_bitcast_fusion.1
  414.7 4.4 fusion.151
  419.1 4.7 fusion.133
  425.5 3.9 convolution_bitcast_fusion
  431.1 7.4 convert_reduce_fusion
  439.9 4.4 convolution_bitcast_fusion.2
  445.9 6.8 convert_reduce_fusion.1
  454.2 4.5 convolution_bitcast_fusion.3
  460.2 4.0 fusion.252
  464.2 2.7 add_bitcast_fusion.1
  467.0 4.1 fusion.251
  471.1 2.8 add_bitcast_fusion.2
  475.3 3.6 fusion.68
  478.9 3.6 fusion.88
  482.6 4.8 fusion.64
  487.4 4.5 fusion.80
  492.2 16.0 %all-reduce.5 = (f32[768]{0:T(1024)}, f32[1024]{0:T(1024)}) all-reduce(f32[768]{0:T(1024)S(1)} %add.401, f32[1024]{0:T(1024)S(1)} %add.402), channel_id=1, replica_groups=mesh['dp'=8,'tensor'=4] {'dp'}, use_global_device_ids=true, to_apply=%region_36.37 | all-reduce | flops 1792 | bytes 14336 | tf_op jit(solution)/shard_map/psum | solution.py:265
  509.8 2.0 copy.58
  511.8 39.2 %reduce-scatter.15.cloned.1.call-done = f32[1,256,1024]{2,1,0:T(8,128)} async-done(((f32[1,1024,1024]{2,1,0:T(8,128)}), f32[1,256,1024]{2,1,0:T(8,128)}) %reduce-scatter.15.cloned.1.call-update) | async-done | bytes 1048592 | tf_op jit(solution)/shard_map/reduce_scatter | solution.py:248
  551.1 79.6 %reduce-scatter.19.cloned.1.call-done = f32[1,256,1024]{2,1,0:T(8,128)} async-done(((f32[1,1024,1024]{2,1,0:T(8,128)}), f32[1,256,1024]{2,1,0:T(8,128)}) %reduce-scatter.19.cloned.1.call-update) | async-done | bytes 1048592 | tf_op jit(solution)/shard_map/reduce_scatter | solution.py:248
  630.6 2.0 fusion.177
  632.7 77.5 %reduce-scatter.21.cloned.1.call-done = f32[1,256,1024]{2,1,0:T(8,128)} async-done(((f32[1,1024,1024]{2,1,0:T(8,128)}), f32[1,256,1024]{2,1,0:T(8,128)}) %reduce-scatter.21.cloned.1.call-update) | async-done | bytes 1048592 | tf_op jit(solution)/shard_map/reduce_scatter | solution.py:249
  710.2 79.4 %reduce-scatter.17.cloned.1.call-done = f32[1,256,1024]{2,1,0:T(8,128)} async-done(((f32[1,1024,1024]{2,1,0:T(8,128)}), f32[1,256,1024]{2,1,0:T(8,128)}) %reduce-scatter.17.cloned.1.call-update) | async-done | bytes 1048592 | tf_op jit(solution)/shard_map/reduce_scatter | solution.py:249
  789.7 3.2 fusion.178
  795.8 44.0 %all-reduce.4 = (f32[1024]{0:T(1024)}, f32[1024]{0:T(1024)}, f32[1024]{0:T(1024)}, f32[1024]{0:T(1024)}, f32[1024]{0:T(1024)S(1)}) all-reduce(f32[1024]{0:T(1024)S(1)} %add.403, f32[1024]{0:T(1024)S(1)} %add.404, f32[1024]{0:T(1024)S(1)} %add.405, f32[1024]{0:T(1024)S(1)} %add.406, ...), channel_id=1, replica_groups=mesh['dp'=8,'tensor'=4] {'dp','tensor'}, use_global_device_ids=true, to_apply=%region_42.43 | all-reduce | flops 5120 | bytes 40960 | tf_op jit(solution)/shard_map/psum | solution.py:266
  839.8 30.5 %reduce-scatter.13.cloned.1.call-done = f32[1,256,1024]{2,1,0:T(8,128)} async-done(((f32[1,1024,1024]{2,1,0:T(8,128)}), f32[1,256,1024]{2,1,0:T(8,128)}) %reduce-scatter.13.cloned.1.call-update) | async-done | bytes 1048592 | tf_op jit(solution)/shard_map/reduce_scatter | solution.py:159
  870.2 79.4 %reduce-scatter.11.cloned.1.call-done = f32[1,256,1024]{2,1,0:T(8,128)} async-done(((f32[1,1024,1024]{2,1,0:T(8,128)}), f32[1,256,1024]{2,1,0:T(8,128)}) %reduce-scatter.11.cloned.1.call-update) | async-done | bytes 1048592 | tf_op jit(solution)/shard_map/reduce_scatter | solution.py:159
  949.6 2.7 fusion.181
  954.9 45.7 %reduce-scatter.23.cloned.1.call-done = f32[128,768]{1,0:T(8,128)} async-done(((f32[1024,768]{1,0:T(8,128)}), f32[128,768]{1,0:T(8,128)}) %reduce-scatter.23.cloned.1.call-update) | async-done | bytes 393232 | tf_op jit(solution)/shard_map/reduce_scatter | solution.py:260
  1000.6 55.3 %reduce-scatter.27.cloned.1.call-done = f32[128,1024]{1,0:T(8,128)} async-done(((f32[1024,1024]{1,0:T(8,128)}), f32[128,1024]{1,0:T(8,128)}) %reduce-scatter.27.cloned.1.call-update) | async-done | bytes 524304 | tf_op jit(solution)/shard_map/reduce_scatter | solution.py:262
  (415 shorter events, 83.8 us)
Async XLA Ops:
  7.2 8.5 copy-start.16
  7.2 32.6 %all-gather.12.cloned.1.call-start = ((), (), s32[]{:S(2)}) async-start(), calls=%async_computation.11 | async-start | bytes 1769472 | tf_op jit(solution)/shard_map/all_gather | solution.py:101
  7.9 79.9 %all-gather.10.cloned.1.call-start = ((), (), s32[]{:S(2)}) async-start(), calls=%async_computation.10 | async-start | bytes 2621440 | tf_op jit(solution)/shard_map/all_gather | solution.py:97
  9.4 5.4 copy-start.92
  11.6 8.6 copy-start.105
  11.7 11.8 %copy-start.89 = (s32[2,1024]{1,0:T(2,128)S(1)}, s32[2,1024]{1,0:T(2,128)}, u32[]{:S(2)}) copy-start(s32[2,1024]{1,0:T(2,128)} %param.43) | copy-start | bytes 24580
  11.7 12.8 %copy-start.88 = (bf16[128,256]{1,0:T(8,128)(2,1)S(1)}, bf16[128,256]{1,0:T(8,128)(2,1)}, u32[]{:S(2)}) copy-start(bf16[128,256]{1,0:T(8,128)(2,1)} %param.50) | copy-start | bytes 196612
  14.8 73.0 %copy-start.113 = (f32[768]{0:T(1024)S(1)}, f32[768]{0:T(1024)}, u32[]{:S(2)}) copy-start(f32[768]{0:T(1024)} %param.49) | copy-start | bytes 9220
  14.9 119.2 %all-gather.20.cloned.1.call-start = ((), (), s32[]{:S(2)}) async-start(), calls=%async_computation.16 | async-start | bytes 2621440 | tf_op jit(solution)/shard_map/all_gather | solution.py:97
  15.6 164.6 %all-gather.24.cloned.1.call-start = ((), (), s32[]{:S(2)}) async-start(), calls=%async_computation.19 | async-start | bytes 2621440 | tf_op jit(solution)/shard_map/all_gather | solution.py:162
  16.8 209.5 %all-gather.26.cloned.1.call-start = ((), (), s32[]{:S(2)}) async-start(), calls=%async_computation.22 | async-start | bytes 2621440 | tf_op jit(solution)/shard_map/all_gather | solution.py:162
  17.4 255.6 %all-gather.22.cloned.1.call-start = ((), (), s32[]{:S(2)}) async-start(), calls=%async_computation.17 | async-start | bytes 2621440 | tf_op jit(solution)/shard_map/all_gather | solution.py:98
  18.0 283.6 %all-gather.16.cloned.1.call-start = ((), (), s32[]{:S(2)}) async-start(), calls=%async_computation.13 | async-start | bytes 2359296 | tf_op jit(solution)/shard_map/all_gather | solution.py:103
  18.7 330.9 %all-gather.14.cloned.1.call-start = ((), (), s32[]{:S(2)}) async-start(), calls=%async_computation.12 | async-start | bytes 2621440 | tf_op jit(solution)/shard_map/all_gather | solution.py:98
  19.5 410.0 %all-gather.18.cloned.1.call-start = ((), (), s32[]{:S(2)}) async-start(), calls=%async_computation.14 | async-start | bytes 2359296 | tf_op jit(solution)/shard_map/all_gather | solution.py:104
  20.2 487.9 %reduce-scatter.25.cloned.1.call-start = ((), (), s32[]{:S(2)}) async-start(), calls=%async_computation.26 | async-start | bytes 1179648 | tf_op jit(solution)/shard_map/reduce_scatter | solution.py:261
  37.2 189.1 %copy-start.21 = (bf16[1024,256]{1,0:T(8,128)(2,1)}, bf16[1024,256]{1,0:T(8,128)(2,1)S(1)}, u32[]{:S(2)}) copy-start(bf16[1024,256]{1,0:T(8,128)(2,1)S(1)} %all_gather.44) | copy-start | bytes 1572868
  37.6 173.3 %copy-start.7 = (pred[512,1024]{1,0:T(8,128)(4,1)}, pred[512,1024]{1,0:T(8,128)(4,1)S(1)}, u32[]{:S(2)}) copy-start(pred[512,1024]{1,0:T(8,128)(4,1)S(1)} %compare_and_fusion) | copy-start | bytes 1572868
  38.0 202.7 %copy-start.10 = (pred[512,1024]{1,0:T(8,128)(4,1)}, pred[512,1024]{1,0:T(8,128)(4,1)S(1)}, u32[]{:S(2)}) copy-start(pred[512,1024]{1,0:T(8,128)(4,1)S(1)} %compare_and_fusion.1) | copy-start | bytes 1572868
  38.6 148.7 %copy-start.5 = (pred[512,768]{1,0:T(8,128)(4,1)}, pred[512,768]{1,0:T(8,128)(4,1)S(1)}, u32[]{:S(2)}) copy-start(pred[512,768]{1,0:T(8,128)(4,1)S(1)} %get-tuple-element.314) | copy-start | bytes 1179652
  143.6 49.2 %copy-start.60 = (bf16[1,1024,4,16]{1,3,2,0:T(8,128)(2,1)}, bf16[1,1024,4,16]{1,3,2,0:T(8,128)(2,1)S(1)}, u32[]{:S(2)}) copy-start(bf16[1,1024,4,16]{1,3,2,0:T(8,128)(2,1)S(1)} %get-tuple-element.271) | copy-start | bytes 393220
  143.6 63.4 %copy-start.58 = (bf16[1,1024,4,16]{1,3,2,0:T(8,128)(2,1)}, bf16[1,1024,4,16]{1,3,2,0:T(8,128)(2,1)S(1)}, u32[]{:S(2)}) copy-start(bf16[1,1024,4,16]{1,3,2,0:T(8,128)(2,1)S(1)} %get-tuple-element.273) | copy-start | bytes 393220
  147.8 39.6 %copy-start.80 = (f32[4,512]{1,0:T(4,128)}, f32[4,512]{1,0:T(4,128)S(1)}, u32[]{:S(2)}) copy-start(f32[4,512]{1,0:T(4,128)S(1)} %log_add_fusion.3) | copy-start | bytes 24580
  182.6 5.2 slice-start.1
  201.5 5.5 copy-start.19
  215.9 17.9 %copy-start.23 = (bf16[1,4,1024,64]{2,3,1,0:T(8,128)(2,1)}, bf16[1,4,1024,64]{2,3,1,0:T(8,128)(2,1)S(1)}, u32[]{:S(2)}) copy-start(bf16[1,4,1024,64]{2,3,1,0:T(8,128)(2,1)S(1)} %maximum_convert_fusion.2) | copy-start | bytes 1572868
  215.9 17.9 %copy-start.25 = (bf16[1,4,1024,64]{2,3,1,0:T(8,128)(2,1)}, bf16[1,4,1024,64]{2,3,1,0:T(8,128)(2,1)S(1)}, u32[]{:S(2)}) copy-start(bf16[1,4,1024,64]{2,3,1,0:T(8,128)(2,1)S(1)} %maximum_convert_fusion.3) | copy-start | bytes 1572868
  226.3 5.7 copy-start.43
  233.8 7.0 slice-start.8
  234.4 6.4 slice-start.9
  251.6 258.2 %reduce-scatter.29.cloned.1.call-start = ((), (), s32[]{:S(2)}) async-start(), calls=%async_computation.28 | async-start | bytes 4718592 | tf_op jit(solution)/shard_map/reduce_scatter | solution.py:263
  349.6 23.9 %copy-start.41 = (bf16[1,1024,1024]{2,1,0:T(8,128)(2,1)S(1)}, bf16[1,1024,1024]{2,1,0:T(8,128)(2,1)}, u32[]{:S(2)}) copy-start(bf16[1,1024,1024]{2,1,0:T(8,128)(2,1)} %all-gather.26.cloned.1.call-done) | copy-start | bytes 6291460
  381.2 169.8 %reduce-scatter.15.cloned.1.call-start = ((), (), s32[]{:S(2)}) async-start(), calls=%async_computation.20 | async-start | bytes 5242880 | tf_op jit(solution)/shard_map/reduce_scatter | solution.py:248
  381.3 7.1 copy-start.8
  381.3 7.1 copy-start.66
  381.3 7.1 copy-start.84
  385.4 9.6 slice-start.6
  388.4 6.6 slice-start.7
  408.1 5.0 copy-start.50
  413.1 217.5 %reduce-scatter.19.cloned.1.call-start = ((), (), s32[]{:S(2)}) async-start(), calls=%async_computation.23 | async-start | bytes 5242880 | tf_op jit(solution)/shard_map/reduce_scatter | solution.py:248
  429.4 280.8 %reduce-scatter.21.cloned.1.call-start = ((), (), s32[]{:S(2)}) async-start(), calls=%async_computation.24 | async-start | bytes 5242880 | tf_op jit(solution)/shard_map/reduce_scatter | solution.py:249
  431.1 8.7 copy-start.109
  444.3 345.3 %reduce-scatter.17.cloned.1.call-start = ((), (), s32[]{:S(2)}) async-start(), calls=%async_computation.21 | async-start | bytes 5242880 | tf_op jit(solution)/shard_map/reduce_scatter | solution.py:249
  445.9 8.3 copy-start.110
  458.7 5.5 copy-start.22
  458.7 5.5 copy-start.26
  458.7 411.6 %reduce-scatter.13.cloned.1.call-start = ((), (), s32[]{:S(2)}) async-start(), calls=%async_computation.18 | async-start | bytes 5242880 | tf_op jit(solution)/shard_map/reduce_scatter | solution.py:159
  467.0 482.6 %reduce-scatter.11.cloned.1.call-start = ((), (), s32[]{:S(2)}) async-start(), calls=%async_computation.15 | async-start | bytes 5242880 | tf_op jit(solution)/shard_map/reduce_scatter | solution.py:159
  473.9 526.7 %reduce-scatter.23.cloned.1.call-start = ((), (), s32[]{:S(2)}) async-start(), calls=%async_computation.25 | async-start | bytes 3538944 | tf_op jit(solution)/shard_map/reduce_scatter | solution.py:260
  482.5 573.3 %reduce-scatter.27.cloned.1.call-start = ((), (), s32[]{:S(2)}) async-start(), calls=%async_computation.27 | async-start | bytes 4718592 | tf_op jit(solution)/shard_map/reduce_scatter | solution.py:262
  492.0 138.7 %copy-start.4 = (bf16[2,256,1024]{2,1,0:T(8,128)(2,1)S(1)}, bf16[2,256,1024]{2,1,0:T(8,128)(2,1)}, u32[]{:S(2)}) copy-start(bf16[2,256,1024]{2,1,0:T(8,128)(2,1)} %param.40) | copy-start | bytes 3145732
  492.0 138.7 %copy-start.83 = (f32[1024]{0:T(1024)S(1)}, f32[1024]{0:T(1024)}, u32[]{:S(2)}) copy-start(f32[1024]{0:T(1024)} %param.44) | copy-start | bytes 12292
  492.0 138.7 %copy-start.91 = (f32[256]{0:T(256)S(1)}, f32[256]{0:T(256)}, u32[]{:S(2)}) copy-start(f32[256]{0:T(256)} %copy-done.90) | copy-start | bytes 3076
  492.0 138.7 %copy-start.93 = (f32[256]{0:T(256)S(1)}, f32[256]{0:T(256)}, u32[]{:S(2)}) copy-start(f32[256]{0:T(256)} %copy-done.92) | copy-start | bytes 3076
  492.0 140.7 %copy-start.101 = (f32[256]{0:T(256)S(1)}, f32[256]{0:T(256)}, u32[]{:S(2)}) copy-start(f32[256]{0:T(256)} %copy-done.100) | copy-start | bytes 3076
  492.0 140.7 %copy-start.99 = (f32[256]{0:T(256)S(1)}, f32[256]{0:T(256)}, u32[]{:S(2)}) copy-start(f32[256]{0:T(256)} %copy-done.98) | copy-start | bytes 3076
  492.0 297.6 %copy-start.82 = (f32[1024]{0:T(1024)S(1)}, f32[1024]{0:T(1024)}, u32[]{:S(2)}) copy-start(f32[1024]{0:T(1024)} %param.46) | copy-start | bytes 12292
  492.0 297.6 %copy-start.95 = (f32[256]{0:T(256)S(1)}, f32[256]{0:T(256)}, u32[]{:S(2)}) copy-start(f32[256]{0:T(256)} %copy-done.94) | copy-start | bytes 3076
  492.0 297.6 %copy-start.97 = (f32[256]{0:T(256)S(1)}, f32[256]{0:T(256)}, u32[]{:S(2)}) copy-start(f32[256]{0:T(256)} %copy-done.96) | copy-start | bytes 3076
  710.2 82.8 %copy-start.14 = (f32[1,256,1024]{2,1,0:T(8,128)S(1)}, f32[1,256,1024]{2,1,0:T(8,128)}, u32[]{:S(2)}) copy-start(f32[1,256,1024]{2,1,0:T(8,128)} %reduce-scatter.21.cloned.1.call-done) | copy-start | bytes 3145732
  792.9 156.7 %copy-start.13 = (f32[1,256,1024]{2,1,0:T(8,128)S(1)}, f32[1,256,1024]{2,1,0:T(8,128)}, u32[]{:S(2)}) copy-start(f32[1,256,1024]{2,1,0:T(8,128)} %reduce-scatter.19.cloned.1.call-done) | copy-start | bytes 3145732
  792.9 156.7 %copy-start.102 = (f32[1024]{0:T(1024)S(1)}, f32[1024]{0:T(1024)}, u32[]{:S(2)}) copy-start(f32[1024]{0:T(1024)} %param.55) | copy-start | bytes 12292
  792.9 156.7 %copy-start.103 = (f32[1024]{0:T(1024)S(1)}, f32[1024]{0:T(1024)}, u32[]{:S(2)}) copy-start(f32[1024]{0:T(1024)} %param.51) | copy-start | bytes 12292
  839.7 216.1 %copy-start.104 = (f32[1024]{0:T(1024)}, f32[1024]{0:T(1024)S(1)}, u32[]{:S(2)}) copy-start(f32[1024]{0:T(1024)S(1)} %get-tuple-element.342) | copy-start | bytes 12292
  (87 other events, 239.8 us)
Sparse Core Ops, SparseCore 0:
  9.9 29.7 all-gather.11
  41.9 45.9 all-gather.9
  89.4 44.6 all-gather.19
  135.5 44.6 all-gather.23
  181.6 44.6 all-gather.25
  228.3 44.6 all-gather.21
  274.9 26.5 all-gather.15
  303.7 45.9 all-gather.13
  351.5 26.6 all-gather.17
  381.2 36.0 reduce-scatter.24
  420.7 51.3 reduce-scatter.28
  474.3 76.7 reduce-scatter.14
  553.4 77.2 reduce-scatter.18
  632.9 77.2 reduce-scatter.20
  712.3 77.2 reduce-scatter.16
  791.9 78.3 reduce-scatter.12
  872.4 77.2 reduce-scatter.10
  953.8 46.7 reduce-scatter.22
  1004.5 51.2 reduce-scatter.26
where the time goes:
time: 1070 us; the launch traced here: 1060 us
  waiting for transfers between devices  709 us (66%)
  matrix products  181 us (17%)
  blocking collectives  72.7 us (7%)
  other arithmetic  48.3 us (5%)
  local copies, waits for them, and re-layouts  35.3 us (3%)
  between operations  16.4 us (2%)
    reduce_scatter x2, waiting for transfers between devices, on_device(): lax.psum_scatter(grad_two, 'tensor', scatter_dimension=1, tiled=True)  157 us
    reduce_scatter x2, waiting for transfers between devices, on_device(): lax.psum_scatter(grad_one, 'tensor', scatter_dimension=1, tiled=True)  119 us
    reduce_scatter x2, waiting for transfers between devices, on_device(): lax.psum_scatter(partial_sum, 'tensor', scatter_dimension=1, tiled=True)  110 us
    all_gather x2, waiting for transfers between devices, on_device(): lax.all_gather(value_one.astype(jnp.bfloat16), 'tensor', axis=1, tiled=True)  85.3 us
    all_gather x2, waiting for transfers between devices, on_device(): lax.all_gather(value_two.astype(jnp.bfloat16), 'tensor', axis=1, tiled=True)  62.8 us
    reduce_scatter x1, waiting for transfers between devices, on_device(): lax.psum_scatter(grad_upw, 'dp', scatter_dimension=0, tiled=True)  55.3 us
    reduce_scatter x1, waiting for transfers between devices, on_device(): lax.psum_scatter(grad_qkv, 'dp', scatter_dimension=0, tiled=True)  45.7 us
    psum x1, blocking collectives, on_device(): lax.psum((sum_gain_one, sum_bias_one, sum_gain_two, sum_bias_two, sum_slo...  44 us
  transfers between devices with their start and end apart: 19, of which 16 were waited for; matrix products, arithmetic and copies ran while one was open for 23% of the time, Pallas kernels for 0%

commit v1 on v0

--- a/solution.py
+++ b/solution.py
@@ -7,6 +7,16 @@
 ROT = 16
 BLOCK = 256
 MICRO = 2
+
+
+def turned_line(block, name, dim):
+    size = lax.axis_size(name)
+    held, blocks = (block, [block])
+    for _ in range(size - 1):
+        held = lax.ppermute(held, name, [(i, (i + 1) % size) for i in range(size)])
+        blocks.insert(0, held)
+    line = jnp.concatenate(blocks, axis=dim)
+    return jnp.roll(line, (lax.axis_index(name) + 1) * block.shape[dim], axis=dim)
 
 
 def layer_norm(values, ln_gain, ln_bias):
@@ -159,7 +169,7 @@
         reduced = lax.psum_scatter(partial_sum, "tensor", scatter_dimension=1, tiled=True)
         out_rows.append((residual + reduced + b_out + b_down).astype(jnp.bfloat16))
         slope_local = cotangent[first_seq:last_seq]
-        slope = lax.all_gather(slope_local, "tensor", axis=1, tiled=True)
+        slope = turned_line(slope_local, "tensor", 1)
         qkv_full, out_full, up_full, down_full = (
             lax.all_gather(w_qkv, "dp", axis=0, tiled=True),
             lax.all_gather(w_out, "dp", axis=0, tiled=True),

time: 1070 us -> 1010 us (0.944)
  waiting for transfers between devices: 709 us -> 607 us
  other arithmetic: 48.3 us -> 80 us
  starting transfers between devices: 1.4 us -> 21.9 us
    reduce_scatter x2, waiting for transfers between devices: 119 us -> 26.8 us  [on_device(): lax.psum_scatter(grad_one, 'tensor', scatter_dimension=1, tiled=True)]
    all_gather x2, waiting for transfers between devices: 85.3 us -> 20.4 us  [on_device(): lax.all_gather(value_one.astype(jnp.bfloat16), 'tensor', axis=1, tiled=True)]
    ppermute x0 -> x6, waiting for transfers between devices: none -> 62 us  [turned_line(): held = lax.ppermute(held, name, [(i, (i + 1) % size) for i in range(size)])]
    reduce_scatter x1, waiting for transfers between devices: 0.01 us -> 55.1 us  [on_device(): lax.psum_scatter(grad_downw, 'dp', scatter_dimension=0, tiled=True)]
    all_gather x2, waiting for transfers between devices: 62.8 us -> 9.45 us  [on_device(): lax.all_gather(value_two.astype(jnp.bfloat16), 'tensor', axis=1, tiled=True)]
    all_gather x2 -> x0, waiting for transfers between devices: 40 us -> none  [on_device(): slope = lax.all_gather(slope_local, 'tensor', axis=1, tiled=True)]
    reduce_scatter x1, waiting for transfers between devices: 0.01 us -> 34.9 us  [on_device(): lax.psum_scatter(grad_outw, 'dp', scatter_dimension=0, tiled=True)]
    all_gather x1, waiting for transfers between devices: 28.5 us -> 0.02 us  [on_device(): lax.all_gather(w_up, 'dp', axis=0, tiled=True)]
  transfers between devices with their start and end apart: 19 -> 23, of which waited for: 16 -> 17; matrix products, arithmetic and copies ran while one was open for 23% -> 27% of each run, Pallas kernels for 0% -> 0%
where the time goes in v1:
time: 1010 us; the launch traced here: 1000 us
  waiting for transfers between devices  607 us (60%)
  matrix products  183 us (18%)
  other arithmetic  80 us (8%)
  blocking collectives  69.7 us (7%)
  local copies, waits for them, and re-layouts  26.5 us (3%)
  starting transfers between devices  21.9 us (2%)
  between operations  16.4 us (2%)
    reduce_scatter x2, waiting for transfers between devices, on_device(): lax.psum_scatter(grad_two, 'tensor', scatter_dimension=1, tiled=True)  157 us
    reduce_scatter x2, waiting for transfers between devices, on_device(): lax.psum_scatter(partial_sum, 'tensor', scatter_dimension=1, tiled=True)  110 us
    ppermute x6, waiting for transfers between devices, turned_line(): held = lax.ppermute(held, name, [(i, (i + 1) % size) for i in range(size)])  62 us
    reduce_scatter x1, waiting for transfers between devices, on_device(): lax.psum_scatter(grad_upw, 'dp', scatter_dimension=0, tiled=True)  55.5 us
    reduce_scatter x1, waiting for transfers between devices, on_device(): lax.psum_scatter(grad_downw, 'dp', scatter_dimension=0, tiled=True)  55.1 us
    reduce_scatter x1, waiting for transfers between devices, on_device(): lax.psum_scatter(grad_qkv, 'dp', scatter_dimension=0, tiled=True)  50.1 us
    psum x1, blocking collectives, on_device(): lax.psum((sum_gain_one, sum_bias_one, sum_gain_two, sum_bias_two, sum_slo...  43.8 us
    reduce_scatter x1, waiting for transfers between devices, on_device(): lax.psum_scatter(grad_outw, 'dp', scatter_dimension=0, tiled=True)  34.9 us
  transfers between devices with their start and end apart: 23, of which 17 were waited for; matrix products, arithmetic and copies ran while one was open for 27% of the time, Pallas kernels for 0%

profile of v1, /device:TPU:0, one launch (start us, length us, event | category | flops | bytes accessed | tf_op | source)
XLA Modules:
  0.0 1004.7 jit_solution(11192283898111539397)
XLA Ops:
  11.6 3.1 fusion.155
  17.4 3.1 collective-permute-start
  24.1 10.9 %all_gather.18 = bf16[1024,256]{1,0:T(8,128)(2,1)S(1)} all-gather(bf16[128,256]{1,0:T(8,128)(2,1)S(1)} %copy-done.91), channel_id=1, replica_groups=mesh['dp'=8,'tensor'=4] {'dp'}, dimensions={0}, use_global_device_ids=true | all-gather | bytes 589824 | tf_op jit(solution)/shard_map/all_gather | solution.py:112
  38.9 7.7 collective-permute-done.3
  46.7 16.1 %collective-permute-done.1 = bf16[1,256,1024]{2,1,0:T(8,128)(2,1)} collective-permute-done((bf16[1,256,1024]{2,1,0:T(8,128)(2,1)S(1)}, bf16[1,256,1024]{2,1,0:T(8,128)(2,1)}, u32[]{:S(2)}, u32[]{:S(2)}) %collective-permute-start.1) | collective-permute-done | bytes 524320 | tf_op jit(solution)/shard_map/ppermute | solution.py:16
  62.8 4.4 collective-permute-start.2
  68.9 16.3 %collective-permute-done.4 = bf16[1,256,1024]{2,1,0:T(8,128)(2,1)} collective-permute-done((bf16[1,256,1024]{2,1,0:T(8,128)(2,1)}, bf16[1,256,1024]{2,1,0:T(8,128)(2,1)}, u32[]{:S(2)}, u32[]{:S(2)}) %collective-permute-start.4) | collective-permute-done | bytes 524320 | tf_op jit(solution)/shard_map/ppermute | solution.py:16
  85.3 9.6 collective-permute-start.5
  94.9 12.8 %collective-permute-done.2 = bf16[1,256,1024]{2,1,0:T(8,128)(2,1)} collective-permute-done((bf16[1,256,1024]{2,1,0:T(8,128)(2,1)}, bf16[1,256,1024]{2,1,0:T(8,128)(2,1)}, u32[]{:S(2)}, u32[]{:S(2)}) %collective-permute-start.2) | collective-permute-done | bytes 524320 | tf_op jit(solution)/shard_map/ppermute | solution.py:16
  107.7 6.1 fusion.56
  115.5 9.0 collective-permute-done.5
  124.4 9.7 fusion.48
  137.0 3.9 fusion.79
  146.1 20.4 %all-gather.18.cloned.1.call-done = bf16[1,1024,1024]{2,1,0:T(8,128)(2,1)} async-done(((bf16[1,256,1024]{2,1,0:T(8,128)(2,1)}), bf16[1,1024,1024]{2,1,0:T(8,128)(2,1)}) %all-gather.18.cloned.1.call-update) | async-done | bytes 2097168 | tf_op jit(solution)/shard_map/all_gather | solution.py:107
  166.5 3.9 fusion.85
  179.3 2.5 multiply_reduce_fusion.3
  191.3 4.7 multiply_reduce_fusion.1
  196.1 3.1 multiply_convert_fusion.1
  199.3 2.9 fusion.140
  207.2 4.2 multiply_reduce_fusion.2
  211.4 4.0 multiply_convert_fusion.2
  223.0 7.2 multiply_reduce_fusion
  230.3 6.4 multiply_convert_fusion
  236.6 3.8 fusion.141
  252.3 3.8 convolution_bitcast_fusion.1
  257.6 4.5 fusion.133
  262.1 5.2 fusion.121
  269.5 3.9 convolution_bitcast_fusion
  273.5 6.7 fusion.62
  280.1 9.4 all-gather.12.cloned.1.call-done
  289.6 6.5 fusion.70
  296.1 22.0 %all-gather.16.cloned.1.call-done = bf16[1024,1024]{1,0:T(8,128)(2,1)} async-done(((bf16[128,1024]{1,0:T(8,128)(2,1)}), bf16[1024,1024]{1,0:T(8,128)(2,1)}) %all-gather.16.cloned.1.call-update) | async-done | bytes 2097168 | tf_op jit(solution)/shard_map/all_gather | solution.py:114
  318.1 4.1 fusion.235
  323.4 24.4 %convert_reduce_fusion.1 = (f32[1024]{0:T(1024)S(1)}, bf16[1024,1024]{1,0:T(8,128)(2,1)}, f32[1024,1024]{1,0:T(8,128)}, f32[1024]{0:T(1024)S(1)}, bf16[1024,1024]{1,0:T(8,128)(2,1)S(1)}, /*index=5*/f32[1024,1024]{1,0:T(8,128)}) fusion(f32[1024,1024]{1,0:T(8,128)S(1)} %copy-done.41, f32[1024]{0:T(1024)S(1)} %copy-done.118, f32[1024,1024]{1,0:T(8,128)S(1)} %fusion.235, ...), kind=kOutput, calls=%fused_computation.53 | convolution fusion | flops 2304768000 | bytes 29372416 | tf_op jit(solution)/shard_map/bsd,df->bsf/dot_general | solution.py:189
  349.1 4.3 convolution_bitcast_fusion.2
  353.7 6.0 convolution_bitcast_fusion.3
  360.8 4.6 fusion.143
  365.5 5.2 fusion.137
  370.8 8.3 multiply_convert_fusion.5
  379.1 4.8 fusion.233
  383.9 2.7 add_bitcast_fusion.1
  387.8 4.6 fusion.142
  392.4 5.1 fusion.136
  397.7 2.4 fusion.234
  400.1 2.9 add_bitcast_fusion
  408.0 4.0 fusion.64
  412.1 3.5 fusion.82
  416.0 4.8 fusion.60
  420.8 4.5 fusion.76
  425.4 4.2 fusion.237
  429.7 4.6 convolution_add_fusion
  435.1 15.0 %all-reduce.5 = (f32[768]{0:T(1024)}, f32[1024]{0:T(1024)}) all-reduce(f32[768]{0:T(1024)S(1)} %add.406, f32[1024]{0:T(1024)S(1)} %add.407), channel_id=1, replica_groups=mesh['dp'=8,'tensor'=4] {'dp'}, use_global_device_ids=true, to_apply=%region_36.38 | all-reduce | flops 1792 | bytes 14336 | tf_op jit(solution)/shard_map/psum | solution.py:275
  450.1 26.8 %reduce-scatter.19.cloned.1.call-done = f32[1,256,1024]{2,1,0:T(8,128)} async-done(((f32[1,1024,1024]{2,1,0:T(8,128)}), f32[1,256,1024]{2,1,0:T(8,128)}) %reduce-scatter.19.cloned.1.call-update) | async-done | bytes 1048592 | tf_op jit(solution)/shard_map/reduce_scatter | solution.py:258
  479.0 77.3 %reduce-scatter.21.cloned.1.call-done = f32[1,256,1024]{2,1,0:T(8,128)} async-done(((f32[1,1024,1024]{2,1,0:T(8,128)}), f32[1,256,1024]{2,1,0:T(8,128)}) %reduce-scatter.21.cloned.1.call-update) | async-done | bytes 1048592 | tf_op jit(solution)/shard_map/reduce_scatter | solution.py:259
  556.3 79.7 %reduce-scatter.17.cloned.1.call-done = f32[1,256,1024]{2,1,0:T(8,128)} async-done(((f32[1,1024,1024]{2,1,0:T(8,128)}), f32[1,256,1024]{2,1,0:T(8,128)}) %reduce-scatter.17.cloned.1.call-update) | async-done | bytes 1048592 | tf_op jit(solution)/shard_map/reduce_scatter | solution.py:259
  636.1 3.2 fusion.160
  642.2 43.8 %all-reduce.4 = (f32[1024]{0:T(1024)}, f32[1024]{0:T(1024)}, f32[1024]{0:T(1024)}, f32[1024]{0:T(1024)}, f32[1024]{0:T(1024)S(1)}) all-reduce(f32[1024]{0:T(1024)S(1)} %add.408, f32[1024]{0:T(1024)S(1)} %add.409, f32[1024]{0:T(1024)S(1)} %add.410, f32[1024]{0:T(1024)S(1)} %add.411, ...), channel_id=1, replica_groups=mesh['dp'=8,'tensor'=4] {'dp','tensor'}, use_global_device_ids=true, to_apply=%region_42.44 | all-reduce | flops 5120 | bytes 40960 | tf_op jit(solution)/shard_map/psum | solution.py:276
  686.0 30.5 %reduce-scatter.11.cloned.1.call-done = f32[1,256,1024]{2,1,0:T(8,128)} async-done(((f32[1,1024,1024]{2,1,0:T(8,128)}), f32[1,256,1024]{2,1,0:T(8,128)}) %reduce-scatter.11.cloned.1.call-update) | async-done | bytes 1048592 | tf_op jit(solution)/shard_map/reduce_scatter | solution.py:169
  716.5 79.6 %reduce-scatter.13.cloned.1.call-done = f32[1,256,1024]{2,1,0:T(8,128)} async-done(((f32[1,1024,1024]{2,1,0:T(8,128)}), f32[1,256,1024]{2,1,0:T(8,128)}) %reduce-scatter.13.cloned.1.call-update) | async-done | bytes 1048592 | tf_op jit(solution)/shard_map/reduce_scatter | solution.py:169
  796.2 2.7 fusion.163
  801.4 34.9 %reduce-scatter.25.cloned.1.call-done = f32[128,256]{1,0:T(8,128)} async-done(((f32[1024,256]{1,0:T(8,128)}), f32[128,256]{1,0:T(8,128)}) %reduce-scatter.25.cloned.1.call-update) | async-done | bytes 131088 | tf_op jit(solution)/shard_map/reduce_scatter | solution.py:271
  836.3 50.1 %reduce-scatter.23.cloned.1.call-done = f32[128,768]{1,0:T(8,128)} async-done(((f32[1024,768]{1,0:T(8,128)}), f32[128,768]{1,0:T(8,128)}) %reduce-scatter.23.cloned.1.call-update) | async-done | bytes 393232 | tf_op jit(solution)/shard_map/reduce_scatter | solution.py:270
  886.4 55.5 %reduce-scatter.27.cloned.1.call-done = f32[128,1024]{1,0:T(8,128)} async-done(((f32[1024,1024]{1,0:T(8,128)}), f32[128,1024]{1,0:T(8,128)}) %reduce-scatter.27.cloned.1.call-update) | async-done | bytes 524304 | tf_op jit(solution)/shard_map/reduce_scatter | solution.py:272
  941.9 55.1 %reduce-scatter.29.cloned.1.call-done = f32[128,1024]{1,0:T(8,128)} async-done(((f32[1024,1024]{1,0:T(8,128)}), f32[128,1024]{1,0:T(8,128)}) %reduce-scatter.29.cloned.1.call-update) | async-done | bytes 524304 | tf_op jit(solution)/shard_map/reduce_scatter | solution.py:273
  (412 shorter events, 90.7 us)
Async XLA Ops:
  7.2 10.2 %copy-start.26 = (bf16[2,256,1024]{2,1,0:T(8,128)(2,1)S(1)}, bf16[2,256,1024]{2,1,0:T(8,128)(2,1)}, u32[]{:S(2)}) copy-start(bf16[2,256,1024]{2,1,0:T(8,128)(2,1)} %param.43) | copy-start | bytes 3145732
  7.2 129.8 %all-gather.10.cloned.1.call-start = ((), (), s32[]{:S(2)}) async-start(), calls=%async_computation.11 | async-start | bytes 1769472 | tf_op jit(solution)/shard_map/all_gather | solution.py:111
  7.9 129.1 %all-gather.8.cloned.1.call-start = ((), (), s32[]{:S(2)}) async-start(), calls=%async_computation.10 | async-start | bytes 2621440 | tf_op jit(solution)/shard_map/all_gather | solution.py:107
  9.4 7.9 copy-start.95
  9.4 7.8 copy-start.93
  11.0 6.2 copy-start.111
  11.1 11.1 %copy-start.119 = (s32[2]{0:T(128)S(1)}, s32[2]{0:T(128)}, u32[]{:S(2)}) copy-start(s32[2]{0:T(128)} %param.44) | copy-start | bytes 28
  11.1 13.0 %copy-start.92 = (s32[2,1024]{1,0:T(2,128)S(1)}, s32[2,1024]{1,0:T(2,128)}, u32[]{:S(2)}) copy-start(s32[2,1024]{1,0:T(2,128)} %param.45) | copy-start | bytes 24580
  11.1 13.0 %copy-start.91 = (bf16[128,256]{1,0:T(8,128)(2,1)S(1)}, bf16[128,256]{1,0:T(8,128)(2,1)}, u32[]{:S(2)}) copy-start(bf16[128,256]{1,0:T(8,128)(2,1)} %param.52) | copy-start | bytes 196612
  14.8 151.8 %all-gather.18.cloned.1.call-start = ((), (), s32[]{:S(2)}) async-start(), calls=%async_computation.16 | async-start | bytes 2621440 | tf_op jit(solution)/shard_map/all_gather | solution.py:107
  15.5 257.9 %all-gather.20.cloned.1.call-start = ((), (), s32[]{:S(2)}) async-start(), calls=%async_computation.17 | async-start | bytes 2621440 | tf_op jit(solution)/shard_map/all_gather | solution.py:108
  16.1 257.4 %all-gather.14.cloned.1.call-start = ((), (), s32[]{:S(2)}) async-start(), calls=%async_computation.13 | async-start | bytes 2359296 | tf_op jit(solution)/shard_map/all_gather | solution.py:113
  16.7 272.9 %all-gather.12.cloned.1.call-start = ((), (), s32[]{:S(2)}) async-start(), calls=%async_computation.12 | async-start | bytes 2621440 | tf_op jit(solution)/shard_map/all_gather | solution.py:108
  17.3 300.8 %all-gather.16.cloned.1.call-start = ((), (), s32[]{:S(2)}) async-start(), calls=%async_computation.14 | async-start | bytes 2359296 | tf_op jit(solution)/shard_map/all_gather | solution.py:114
  17.4 50.9 %copy-start.50 = (bf16[1,256,1024]{2,1,0:T(8,128)(2,1)}, bf16[1,256,1024]{2,1,0:T(8,128)(2,1)S(1)}, u32[]{:S(2)}) copy-start(bf16[1,256,1024]{2,1,0:T(8,128)(2,1)S(1)} %get-tuple-element.222) | copy-start | bytes 1572868
  17.4 18.5 %collective-permute-start = (bf16[1,256,1024]{2,1,0:T(8,128)(2,1)S(1)}, bf16[1,256,1024]{2,1,0:T(8,128)(2,1)S(1)}, u32[]{:S(2)}, u32[]{:S(2)}) collective-permute-start(bf16[1,256,1024]{2,1,0:T(8,128)(2,1)S(1)} %get-tuple-element.222), channel_id=1, source_target_pairs={{0,1},{1,2},{2,3},{3,0},{4,5},{5,6},{6,7},{7,4},{8,9},{9,10},{10,1... | collective-permute-start | bytes 1572872 | tf_op jit(solution)/shard_map/ppermute | solution.py:16
  20.5 26.1 %collective-permute-start.3 = (bf16[1,256,1024]{2,1,0:T(8,128)(2,1)S(1)}, bf16[1,256,1024]{2,1,0:T(8,128)(2,1)}, u32[]{:S(2)}, u32[]{:S(2)}) collective-permute-start(bf16[1,256,1024]{2,1,0:T(8,128)(2,1)S(1)} %get-tuple-element.223), channel_id=1, source_target_pairs={{0,1},{1,2},{2,3},{3,0},{4,5},{5,6},{6,7},{7,4},{8,9},{9,10},{10,1... | collective-permute-start | bytes 1572872 | tf_op jit(solution)/shard_map/ppermute | solution.py:16
  22.1 428.0 %reduce-scatter.15.cloned.1.call-start = ((), (), s32[]{:S(2)}) async-start(), calls=%async_computation.19 | async-start | bytes 5242880 | tf_op jit(solution)/shard_map/reduce_scatter | solution.py:258
  35.1 99.1 %copy-start.34 = (bf16[1024,256]{1,0:T(8,128)(2,1)}, bf16[1024,256]{1,0:T(8,128)(2,1)S(1)}, u32[]{:S(2)}) copy-start(bf16[1024,256]{1,0:T(8,128)(2,1)S(1)} %all_gather.18) | copy-start | bytes 1572868
  36.0 32.0 %copy-start.72 = (bf16[1,256,1024]{2,1,0:T(8,128)(2,1)}, bf16[1,256,1024]{2,1,0:T(8,128)(2,1)S(1)}, u32[]{:S(2)}) copy-start(bf16[1,256,1024]{2,1,0:T(8,128)(2,1)S(1)} %collective-permute-done) | copy-start | bytes 1572868
  36.0 26.8 %collective-permute-start.1 = (bf16[1,256,1024]{2,1,0:T(8,128)(2,1)S(1)}, bf16[1,256,1024]{2,1,0:T(8,128)(2,1)}, u32[]{:S(2)}, u32[]{:S(2)}) collective-permute-start(bf16[1,256,1024]{2,1,0:T(8,128)(2,1)S(1)} %collective-permute-done), channel_id=1, source_target_pairs={{0,1},{1,2},{2,3},{3,0},{4,5},{5,6},{6,7},{7,4},{8,9},{9,10},{10,1... | collective-permute-start | bytes 1572872 | tf_op jit(solution)/shard_map/ppermute | solution.py:16
  38.9 223.2 %copy-start.17 = (pred[512,1024]{1,0:T(8,128)(4,1)}, pred[512,1024]{1,0:T(8,128)(4,1)S(1)}, u32[]{:S(2)}) copy-start(pred[512,1024]{1,0:T(8,128)(4,1)S(1)} %compare_and_fusion) | copy-start | bytes 1572868
  46.6 38.6 %collective-permute-start.4 = (bf16[1,256,1024]{2,1,0:T(8,128)(2,1)}, bf16[1,256,1024]{2,1,0:T(8,128)(2,1)}, u32[]{:S(2)}, u32[]{:S(2)}) collective-permute-start(bf16[1,256,1024]{2,1,0:T(8,128)(2,1)} %collective-permute-done.3), channel_id=1, source_target_pairs={{0,1},{1,2},{2,3},{3,0},{4,5},{5,6},{6,7},{7,4},{8,9},{9,10},{10,1... | collective-permute-start | bytes 1572872 | tf_op jit(solution)/shard_map/ppermute | solution.py:16
  62.8 44.9 %collective-permute-start.2 = (bf16[1,256,1024]{2,1,0:T(8,128)(2,1)}, bf16[1,256,1024]{2,1,0:T(8,128)(2,1)}, u32[]{:S(2)}, u32[]{:S(2)}) collective-permute-start(bf16[1,256,1024]{2,1,0:T(8,128)(2,1)} %collective-permute-done.1), channel_id=1, source_target_pairs={{0,1},{1,2},{2,3},{3,0},{4,5},{5,6},{6,7},{7,4},{8,9},{9,10},{10,1... | collective-permute-start | bytes 1572872 | tf_op jit(solution)/shard_map/ppermute | solution.py:16
  68.3 123.0 %copy-start.19 = (pred[512,1024]{1,0:T(8,128)(4,1)}, pred[512,1024]{1,0:T(8,128)(4,1)S(1)}, u32[]{:S(2)}) copy-start(pred[512,1024]{1,0:T(8,128)(4,1)S(1)} %compare_and_fusion.1) | copy-start | bytes 1572868
  68.9 188.6 %copy-start.8 = (pred[512,768]{1,0:T(8,128)(4,1)}, pred[512,768]{1,0:T(8,128)(4,1)S(1)}, u32[]{:S(2)}) copy-start(pred[512,768]{1,0:T(8,128)(4,1)S(1)} %get-tuple-element.272) | copy-start | bytes 1179652
  85.3 39.2 %collective-permute-start.5 = (bf16[1,256,1024]{2,1,0:T(8,128)(2,1)}, bf16[1,256,1024]{2,1,0:T(8,128)(2,1)S(1)}, u32[]{:S(2)}, u32[]{:S(2)}) collective-permute-start(bf16[1,256,1024]{2,1,0:T(8,128)(2,1)} %collective-permute-done.4), channel_id=1, source_target_pairs={{0,1},{1,2},{2,3},{3,0},{4,5},{5,6},{6,7},{7,4},{8,9},{9,10},{10,1... | collective-permute-start | bytes 1572872 | tf_op jit(solution)/shard_map/ppermute | solution.py:16
  115.5 21.5 %copy-start.127 = (f32[768]{0:T(1024)S(1)}, f32[768]{0:T(1024)}, u32[]{:S(2)}) copy-start(f32[768]{0:T(1024)} %param.51) | copy-start | bytes 9220
  176.1 11.4 %copy-start.29 = (bf16[1,4,1024,64]{2,3,1,0:T(8,128)(2,1)}, bf16[1,4,1024,64]{2,3,1,0:T(8,128)(2,1)S(1)}, u32[]{:S(2)}) copy-start(bf16[1,4,1024,64]{2,3,1,0:T(8,128)(2,1)S(1)} %fusion.170) | copy-start | bytes 1572868
  177.4 68.7 %copy-start = (f32[4,512,768]{2,1,0:T(8,128)}, f32[4,512,768]{2,1,0:T(8,128)S(1)}, u32[]{:S(2)}) copy-start(f32[4,512,768]{2,1,0:T(8,128)S(1)} %get-tuple-element.255) | copy-start | bytes 18874372
  189.0 58.8 %copy-start.2 = (f32[4,512,1024]{2,1,0:T(8,128)}, f32[4,512,1024]{2,1,0:T(8,128)S(1)}, u32[]{:S(2)}) copy-start(f32[4,512,1024]{2,1,0:T(8,128)S(1)} %get-tuple-element.253) | copy-start | bytes 25165828
  205.2 6.2 copy-start.85
  205.2 6.2 copy-start.1
  211.4 5.9 copy-start.6
  218.2 22.3 %copy-start.28 = (f32[1,1024,4,64]{1,3,2,0:T(8,128)}, f32[1,1024,4,64]{1,3,2,0:T(8,128)S(1)}, u32[]{:S(2)}) copy-start(f32[1,1024,4,64]{1,3,2,0:T(8,128)S(1)} %fusion.116) | copy-start | bytes 3145732
  220.7 9.6 copy-start.3
  223.0 7.2 copy-start.103
  256.1 220.8 %reduce-scatter.19.cloned.1.call-start = ((), (), s32[]{:S(2)}) async-start(), calls=%async_computation.21 | async-start | bytes 5242880 | tf_op jit(solution)/shard_map/reduce_scatter | solution.py:258
  273.4 282.9 %reduce-scatter.21.cloned.1.call-start = ((), (), s32[]{:S(2)}) async-start(), calls=%async_computation.22 | async-start | bytes 5242880 | tf_op jit(solution)/shard_map/reduce_scatter | solution.py:259
  280.1 38.0 %copy-start.11 = (bf16[1024,1024]{1,0:T(8,128)(2,1)S(1)}, bf16[1024,1024]{1,0:T(8,128)(2,1)}, u32[]{:S(2)}) copy-start(bf16[1024,1024]{1,0:T(8,128)(2,1)} %copy-done.10) | copy-start | bytes 6291460
  296.1 26.1 %copy-start.118 = (f32[1024]{0:T(1024)S(1)}, f32[1024]{0:T(1024)}, u32[]{:S(2)}) copy-start(f32[1024]{0:T(1024)} %param.55) | copy-start | bytes 12292
  323.4 25.8 %copy-start.124 = (bf16[1024,1024]{1,0:T(8,128)(2,1)S(1)}, bf16[1024,1024]{1,0:T(8,128)(2,1)}, u32[]{:S(2)}) copy-start(bf16[1024,1024]{1,0:T(8,128)(2,1)} %all-gather.14.cloned.1.call-done) | copy-start | bytes 6291460
  353.5 282.5 %reduce-scatter.17.cloned.1.call-start = ((), (), s32[]{:S(2)}) async-start(), calls=%async_computation.20 | async-start | bytes 5242880 | tf_op jit(solution)/shard_map/reduce_scatter | solution.py:259
  359.8 356.7 %reduce-scatter.11.cloned.1.call-start = ((), (), s32[]{:S(2)}) async-start(), calls=%async_computation.15 | async-start | bytes 5242880 | tf_op jit(solution)/shard_map/reduce_scatter | solution.py:169
  386.7 5.7 copy-start.18
  386.7 409.4 %reduce-scatter.13.cloned.1.call-start = ((), (), s32[]{:S(2)}) async-start(), calls=%async_computation.18 | async-start | bytes 5242880 | tf_op jit(solution)/shard_map/reduce_scatter | solution.py:169
  403.0 433.4 %reduce-scatter.25.cloned.1.call-start = ((), (), s32[]{:S(2)}) async-start(), calls=%async_computation.24 | async-start | bytes 1179648 | tf_op jit(solution)/shard_map/reduce_scatter | solution.py:271
  408.0 478.4 %reduce-scatter.23.cloned.1.call-start = ((), (), s32[]{:S(2)}) async-start(), calls=%async_computation.23 | async-start | bytes 3538944 | tf_op jit(solution)/shard_map/reduce_scatter | solution.py:270
  415.6 526.3 %reduce-scatter.27.cloned.1.call-start = ((), (), s32[]{:S(2)}) async-start(), calls=%async_computation.25 | async-start | bytes 4718592 | tf_op jit(solution)/shard_map/reduce_scatter | solution.py:272
  425.4 571.7 %reduce-scatter.29.cloned.1.call-start = ((), (), s32[]{:S(2)}) async-start(), calls=%async_computation.26 | async-start | bytes 4718592 | tf_op jit(solution)/shard_map/reduce_scatter | solution.py:273
  434.3 42.6 %copy-start.4 = (bf16[2,256,1024]{2,1,0:T(8,128)(2,1)S(1)}, bf16[2,256,1024]{2,1,0:T(8,128)(2,1)}, u32[]{:S(2)}) copy-start(bf16[2,256,1024]{2,1,0:T(8,128)(2,1)} %param.42) | copy-start | bytes 3145732
  434.3 42.6 %copy-start.82 = (f32[1024]{0:T(1024)S(1)}, f32[1024]{0:T(1024)}, u32[]{:S(2)}) copy-start(f32[1024]{0:T(1024)} %param.46) | copy-start | bytes 12292
  434.3 42.6 %copy-start.94 = (f32[256]{0:T(256)S(1)}, f32[256]{0:T(256)}, u32[]{:S(2)}) copy-start(f32[256]{0:T(256)} %copy-done.93) | copy-start | bytes 3076
  434.3 42.6 %copy-start.96 = (f32[256]{0:T(256)S(1)}, f32[256]{0:T(256)}, u32[]{:S(2)}) copy-start(f32[256]{0:T(256)} %copy-done.95) | copy-start | bytes 3076
  434.3 44.6 %copy-start.114 = (f32[256]{0:T(256)S(1)}, f32[256]{0:T(256)}, u32[]{:S(2)}) copy-start(f32[256]{0:T(256)} %copy-done.113) | copy-start | bytes 3076
  434.3 44.6 %copy-start.112 = (f32[256]{0:T(256)S(1)}, f32[256]{0:T(256)}, u32[]{:S(2)}) copy-start(f32[256]{0:T(256)} %copy-done.111) | copy-start | bytes 3076
  434.3 201.7 %copy-start.81 = (f32[1024]{0:T(1024)S(1)}, f32[1024]{0:T(1024)}, u32[]{:S(2)}) copy-start(f32[1024]{0:T(1024)} %param.48) | copy-start | bytes 12292
  434.3 201.7 %copy-start.106 = (f32[256]{0:T(256)S(1)}, f32[256]{0:T(256)}, u32[]{:S(2)}) copy-start(f32[256]{0:T(256)} %copy-done.105) | copy-start | bytes 3076
  434.4 201.7 %copy-start.108 = (f32[256]{0:T(256)S(1)}, f32[256]{0:T(256)}, u32[]{:S(2)}) copy-start(f32[256]{0:T(256)} %copy-done.107) | copy-start | bytes 3076
  556.3 83.1 %copy-start.24 = (f32[1,256,1024]{2,1,0:T(8,128)S(1)}, f32[1,256,1024]{2,1,0:T(8,128)}, u32[]{:S(2)}) copy-start(f32[1,256,1024]{2,1,0:T(8,128)} %reduce-scatter.21.cloned.1.call-done) | copy-start | bytes 3145732
  639.3 156.9 %copy-start.22 = (f32[1,256,1024]{2,1,0:T(8,128)S(1)}, f32[1,256,1024]{2,1,0:T(8,128)}, u32[]{:S(2)}) copy-start(f32[1,256,1024]{2,1,0:T(8,128)} %reduce-scatter.19.cloned.1.call-done) | copy-start | bytes 3145732
  639.3 156.9 %copy-start.115 = (f32[1024]{0:T(1024)S(1)}, f32[1024]{0:T(1024)}, u32[]{:S(2)}) copy-start(f32[1024]{0:T(1024)} %param.57) | copy-start | bytes 12292
  639.3 156.8 %copy-start.116 = (f32[1024]{0:T(1024)S(1)}, f32[1024]{0:T(1024)}, u32[]{:S(2)}) copy-start(f32[1024]{0:T(1024)} %param.53) | copy-start | bytes 12292
  686.0 311.0 %copy-start.117 = (f32[1024]{0:T(1024)}, f32[1024]{0:T(1024)S(1)}, u32[]{:S(2)}) copy-start(f32[1024]{0:T(1024)S(1)} %get-tuple-element.301) | copy-start | bytes 12292
  (89 other events, 267.7 us)
Sparse Core Ops, SparseCore 0:
  9.9 28.9 all-gather.9
  41.1 79.5 all-gather.7
  122.3 44.2 all-gather.17
  168.5 44.6 all-gather.19
  214.9 26.6 all-gather.13
  243.6 45.9 all-gather.11
  291.4 26.6 all-gather.15
  320.4 76.7 reduce-scatter.14
  399.6 77.2 reduce-scatter.18
  479.0 77.2 reduce-scatter.20
  558.7 77.2 reduce-scatter.16
  638.2 78.2 reduce-scatter.10
  718.9 77.1 reduce-scatter.12
  799.8 36.5 reduce-scatter.24
  840.1 46.2 reduce-scatter.22
  890.5 51.3 reduce-scatter.26
  945.7 51.3 reduce-scatter.28
